TPU v7x, 32 devices: a whole 2x2x4 slice. The times are simulated.
32 devices in a mesh: dom: 8 (over z, y), rep: 4 (over x, core).
Axes of the slice: x: 2, y: 2, z: 4, core: 2. Of those that a mesh axis runs over, the one named last changes fastest.
Arguments:
- node_features: bfloat16 [32768, 128], P(('rep', 'dom')), parts along dimension 0, may hold values from -6 to 6
- edge_features: bfloat16 [86016, 128], P(('rep', 'dom')), parts along dimension 0, may hold values from -6 to 6
- node_cotangent: bfloat16 [32768, 128], P(('rep', 'dom')), parts along dimension 0, may hold values from -6 to 6
- edge_cotangent: bfloat16 [86016, 128], P(('rep', 'dom')), parts along dimension 0, may hold values from -6 to 6
- edge_in_weight: bfloat16 [384, 128], replicated, may hold values from -0.3125 to 0.3125
- edge_in_bias: float32 [128], replicated, may hold values from -3 to 3
- edge_out_weight: bfloat16 [128, 128], replicated, may hold values from -0.5 to 0.5
- edge_out_bias: float32 [128], replicated, may hold values from -3 to 3
- node_in_weight: bfloat16 [256, 128], replicated, may hold values from -0.375 to 0.375
- node_in_bias: float32 [128], replicated, may hold values from -3 to 3
- node_out_weight: bfloat16 [128, 128], replicated, may hold values from -0.5 to 0.5
- edge_ends: int32 [2, 1344], replicated, may hold values from 0 to 511, as said below
- live_elements: int32 [32], P(('rep', 'dom')), parts along dimension 0, may hold values from 1 to 2, as said below
- shared_nodes: int32 [32, 4, 128], P(('rep', 'dom')), parts along dimension 0, may hold values from 0 to 1023, as said below
- shared_counts: int32 [32, 4], P(('rep', 'dom')), parts along dimension 0, may hold values from 32 to 128, as said below
- multiplicity: int32 [32768], P(('rep', 'dom')), parts along dimension 0, may hold values from 1 to 515
Outputs:
- node_gradient: bfloat16 [32768, 128], P(('rep', 'dom')), parts along dimension 0
- edge_gradient: bfloat16 [86016, 128], P(('rep', 'dom')), parts along dimension 0
- edge_in_weight_gradient: float32 [1536, 128], P('rep'), parts along dimension 0
- edge_in_bias_gradient: float32 [512], P('rep'), parts along dimension 0
- edge_out_weight_gradient: float32 [512, 128], P('rep'), parts along dimension 0
- edge_out_bias_gradient: float32 [512], P('rep'), parts along dimension 0
- node_in_weight_gradient: float32 [1024, 128], P('rep'), parts along dimension 0
- node_in_bias_gradient: float32 [512], P('rep'), parts along dimension 0
- node_out_weight_gradient: float32 [512, 128], P('rep'), parts along dimension 0
- node_out_bias_gradient: float32 [512], P('rep'), parts along dimension 0
There are 4 independent parts, one for each index of `rep`. A program takes and returns all parts, laid end to end along the dimension named above; an argument that names none is the same for every part. Nothing has to cross between parts.
Inputs may be any that keep to these rules, and one draw needn't show every extreme that they name: `edge_ends`: each edge joins two nodes next to each other on the element's 8 x 8 x 8 lattice of nodes. `live_elements`: some partition has all 2 slots live. `shared_nodes`: entry s of a partition's list for neighbour k is the node paired with entry s of that neighbour's list for neighbour k xor 1; entries below the count name nodes of live slots; entries at or beyond it are 0. `shared_counts`: both lists of a pair have the same count; some pair has 128 entries.
All inputs are finite; a program needn't handle non-finite values.
Results may differ from a plain program's by a relative error of at most 0.0056.
Values sent between devices are 32-bit elements; how exact they have to be, the bound alone decides.
A program may use at most 64 MiB of HBM per device.

v0:
```python
import functools
import math

import jax
import jax.numpy as jnp
from jax import lax
from jax.experimental import pallas as pl
from jax.experimental.pallas import tpu as pltpu
from jax.sharding import PartitionSpec as P

NPE = 512
LANES = 128
F32 = jnp.float32
BF16 = jnp.bfloat16
MESH = pl.DeviceIdType.MESH


def divisor_up_to(total, cap):
    best = 16
    for size in range(16, cap + 1, 16):
        if total % size == 0:
            best = size
    return best


def mm(left, right):
    return lax.dot_general(left, right, (((1,), (0,)), ((), ())), preferred_element_type=F32)


def mm_rt(left, right):
    return lax.dot_general(left, right, (((1,), (1,)), ((), ())), preferred_element_type=F32)


def mm_lt(left, right):
    return lax.dot_general(left, right, (((0,), (0,)), ((), ())), preferred_element_type=F32)


def halves(value):
    high = value.astype(BF16)
    low = (value - high.astype(F32)).astype(BF16)
    return high, low


def columns_of(row):
    return jnp.transpose(jnp.broadcast_to(row, (LANES, row.shape[1])))


def hits(ids, width):
    lane = lax.broadcasted_iota(jnp.int32, ids.shape, 1).astype(F32)
    tiles = [
        jnp.where(ids == lane + float(LANES * t), 1.0, 0.0).astype(BF16)
        for t in range(width // LANES)
    ]
    return jnp.concatenate(tiles, axis=1)


def activation(linear):
    squashed = 1.0 / (1.0 + jnp.exp(-linear))
    return linear * squashed, squashed * (1.0 + linear * (1.0 - squashed))


def fused(
    n, quarter, edge_scale, node_scale,
    nf_any, ef_any, nc_any, ec_any, wi_any, bi_any, wo_any, bo_any, wn_any, bn_any, wq_any,
    ends_any, live_any, lists_any, counts_any, mult_any,
    ng_any, eg_any, gwi_ref, gbi_ref, gwo_ref, gbo_ref, gwn_ref, gbn_ref, gwq_ref, gbq_ref,
    col_s, col_t, tab_t, tab_tt, pick, pick_t, slope_s, hid_s, eb_s, cot_s, ecot_s,
    inv_s, agg_s, out1, in1, out2, in2,
    nf_ref, ef_ref, nc_ref, ec_ref, wi_ref, bi_ref, wo_ref, bo_ref, wn_ref, bn_ref, wq_ref,
    ends_ref, live_ref, lists_ref, counts_ref, mult_ref, in_sem, ng_ref, eg_ref, out_sem, bias_s, bias_l,
    px_send, px_recv, pair_send, pair_recv, rs_send, rs_recv, ag_send, ag_recv, bs_send, bs_recv,
    *buffers,
):
    nodes = nf_ref.shape[0]
    d = nf_ref.shape[1]
    slots = nodes // NPE
    edges = ends_ref.shape[1]
    me = lax.axis_index("dom")
    rep = lax.axis_index("rep")
    offsets = (1, -1, quarter, -quarter)
    order = _axis_order
    ch = divisor_up_to(edges, 448)
    n_ch = edges // ch

    def device(index):
        return tuple(index if name == "dom" else rep for name in order)

    half = n // 2
    place, parity = me // 2, lax.rem(me, 2)
    kinds = len(buffers) // 4
    parts, pair_land, lands, fulls = (buffers[i * kinds : (i + 1) * kinds] for i in range(4))
    sources = (
        ends_any, nf_any, wi_any, bi_any, ef_any, wo_any, bo_any, counts_any, lists_any,
        mult_any, live_any, wq_any, wn_any, bn_any, nc_any, ec_any,
    )
    targets = (
        ends_ref, nf_ref, wi_ref, bi_ref, ef_ref, wo_ref, bo_ref, counts_ref, lists_ref,
        mult_ref, live_ref, wq_ref, wn_ref, bn_ref, nc_ref, ec_ref,
    )
    loads = [
        pltpu.make_async_copy(source, target, in_sem.at[i])
        for i, (source, target) in enumerate(zip(sources, targets))
    ]
    for load in loads:
        load.start()

    def arrive(first, last):
        for load in loads[first:last]:
            load.wait()

    barrier = pltpu.get_barrier_semaphore()

    def greet(i, carry):
        pl.semaphore_signal(
            barrier, inc=1, device_id=device(lax.rem(me + i, n)), device_id_type=MESH
        )
        return carry

    lax.fori_loop(1, n, greet, 0)

    arrive(0, 1)
    ends = ends_ref[...].astype(F32)
    for start in range(0, edges, LANES):
        stop = min(start + LANES, edges)
        col_s[start:stop, :] = columns_of(ends[0:1, start:stop])
        col_t[start:stop, :] = columns_of(ends[1:2, start:stop])
    arrive(1, 9)
    s_count = lists_ref.shape[1]
    lane_row = lax.broadcasted_iota(jnp.int32, (1, s_count), 1)
    lists = []
    for k in range(4):
        row = jnp.where(lane_row < counts_ref[:, k : k + 1], lists_ref[k : k + 1, :], -1)
        lists.append(row.astype(F32))
    wi = wi_ref[...]
    ef_rows = lambda e, c: pl.ds(pl.multiple_of(e * edges + c * ch, 16), ch)
    nf2 = jnp.concatenate([nf_ref[e * NPE : (e + 1) * NPE, :] for e in range(slots)], axis=1)

    def forward(c, carry):
        rows = pl.ds(pl.multiple_of(c * ch, 16), ch)
        table = hits(col_t[rows, :], NPE)
        tab_t[rows, :] = table
        target = mm(table, nf2).astype(BF16)
        source = mm(hits(col_s[rows, :], NPE), nf2).astype(BF16)
        for e in range(slots):
            span = slice(e * d, (e + 1) * d)
            here = ef_rows(e, c)
            joined = jnp.concatenate([source[:, span], target[:, span], ef_ref[here, :]], axis=1)
            hidden, slope = activation(mm(joined, wi) + bi_ref[...])
            hid_s[here, :] = hidden.astype(BF16)
            slope_s[here, :] = slope
        return carry

    lax.fori_loop(0, n_ch, forward, 0)

    target_row = ends[1:2, :]
    nb = 128
    deg = []
    for b in range(NPE // nb):
        node_id = (lax.broadcasted_iota(jnp.int32, (nb, edges), 0) + b * nb).astype(F32)
        hit = jnp.where(target_row == node_id, 1.0, 0.0)
        tab_tt[b * nb : (b + 1) * nb, :] = hit.astype(BF16)
        deg.append(jnp.sum(hit, axis=1, keepdims=True))
    deg = jnp.concatenate(deg, axis=0)
    stacked = lambda ref: jnp.concatenate(
        [ref[e * edges : (e + 1) * edges, :] for e in range(slots)], axis=1
    )
    wo = wo_ref[...]
    wo2 = jnp.concatenate([wo, wo], axis=0)
    sum_e = mm(tab_tt[...], stacked(ef_ref))
    sum_h = mm(tab_tt[...], stacked(hid_s))
    for e in range(slots):
        span = slice(e * d, (e + 1) * d)
        pair = jnp.concatenate(halves(sum_h[:, span]), axis=1)
        agg_s[e * NPE : (e + 1) * NPE, :] = sum_e[:, span] + mm(pair, wo2) + deg * bo_ref[...]
    for k in range(4):
        pick[k * s_count : (k + 1) * s_count, :] = hits(columns_of(lists[k]), nodes)

    def partner_copies(out, incoming, which):
        return [
            pltpu.make_async_remote_copy(
                src_ref=out.at[k],
                dst_ref=incoming.at[k ^ 1],
                send_sem=px_send.at[which, k],
                recv_sem=px_recv.at[which, k ^ 1],
                device_id=device(lax.rem(me + offsets[k] + n, n)),
                device_id_type=MESH,
            )
            for k in range(4)
        ]

    def send_shared(values, out, incoming, which):
        pair = jnp.concatenate(halves(values), axis=1)
        copies = partner_copies(out, incoming, which)
        for k in range(4):
            both = mm(pick[k * s_count : (k + 1) * s_count, :], pair)
            out[k] = both[:, :d] + both[:, d:]
            copies[k].start()
        return copies

    def take_shared(values, incoming, copies):
        for k in range(4):
            copies[k].wait()
        moved = jnp.concatenate(
            halves(jnp.concatenate([incoming[k] for k in range(4)], axis=0)), axis=1
        )
        both = mm(pick_t[...], moved)
        return values + both[:, :d] + both[:, d:]

    pl.semaphore_wait(barrier, n - 1)
    copies = send_shared(agg_s[...], out1, in1, 0)

    for k in range(4):
        node_id = lax.broadcasted_iota(jnp.int32, (nodes, s_count), 0).astype(F32)
        pick_t[:, k * s_count : (k + 1) * s_count] = jnp.where(
            lists[k] == node_id, 1.0, 0.0
        ).astype(BF16)
    arrive(9, 15)
    mult = mult_ref[...].astype(F32)
    for b in range(nodes // LANES):
        inv_s[b * LANES : (b + 1) * LANES, :] = 1.0 / columns_of(mult[b : b + 1, :])
    live = live_ref[...]
    slot_of = lax.broadcasted_iota(jnp.int32, (nodes, d), 0) // NPE
    node_cot = jnp.where(slot_of < live, nc_ref[...].astype(F32), 0.0)
    cot_n = node_cot.astype(BF16)
    hidden_back = mm_rt(cot_n, wq_ref[...])
    wn = wn_ref[...]
    early = mm(nf_ref[...], wn[:d, :]) + bn_ref[...]
    bias_s[...] = jnp.zeros_like(bias_s)
    bias_s[3:4, :] = jnp.sum(node_cot, axis=0, keepdims=True)

    consistent = (take_shared(agg_s[...], in1, copies) * inv_s[...]).astype(BF16)
    node_hidden, node_slope = activation(early + mm(consistent, wn[d:, :]))
    node_back32 = hidden_back * node_slope
    node_back = node_back32.astype(BF16)
    back = mm_rt(node_back, wn[d:, :]) * inv_s[...]
    agg_s[...] = back
    copies = send_shared(back, out2, in2, 1)

    def pair_copy(which):
        return pltpu.make_async_remote_copy(
            src_ref=parts[which].at[1 - parity],
            dst_ref=pair_land[which],
            send_sem=pair_send.at[0, which],
            recv_sem=pair_recv.at[0, which],
            device_id=device(2 * place + 1 - parity),
            device_id_type=MESH,
        )

    def reduce_copy(which, i):
        peer = lax.rem(place + i, half)
        return pltpu.make_async_remote_copy(
            src_ref=parts[which].at[parity, peer],
            dst_ref=lands[which].at[i - 1],
            send_sem=rs_send.at[which, i - 1],
            recv_sem=rs_recv.at[which, i - 1],
            device_id=device(2 * peer + parity),
            device_id_type=MESH,
        )

    def gather_copy(which, i, slot):
        peer = lax.rem(place + i, half)
        return pltpu.make_async_remote_copy(
            src_ref=fulls[which].at[parity, slot],
            dst_ref=fulls[which].at[parity, slot],
            send_sem=ag_send.at[which, i - 1],
            recv_sem=ag_recv.at[which, i - 1],
            device_id=device(2 * peer + parity),
            device_id_type=MESH,
        )

    def pair_back(which, side):
        return pltpu.make_async_remote_copy(
            src_ref=fulls[which].at[side],
            dst_ref=fulls[which].at[side],
            send_sem=pair_send.at[1, which],
            recv_sem=pair_recv.at[1, which],
            device_id=device(2 * place + 1 - parity),
            device_id_type=MESH,
        )

    def each(step):
        lax.fori_loop(1, half, lambda i, x: (step(i), x)[1], 0)

    def stage_one(which):
        pair_copy(which).start()

    def stage_two(which):
        pair_copy(which).wait()
        parts[which][parity] = parts[which][parity] + pair_land[which][...]
        each(lambda i: reduce_copy(which, i).start())

    def stage_three(which):
        def add(i, total):
            reduce_copy(which, i).wait()
            return total + lands[which][i - 1]

        fulls[which][parity, place] = lax.fori_loop(1, half, add, parts[which][parity, place])
        each(lambda i: gather_copy(which, i, place).start())

    def stage_four(which):
        def one(i):
            gather_copy(which, i, place).wait_send()
            gather_copy(which, i, lax.rem(place - i + half, half)).wait_recv()

        each(one)
        pair_back(which, parity).start()

    def stage_five(which):
        pair_back(which, parity).wait_send()
        pair_back(which, 1 - parity).wait_recv()

    def fill(which, first, value):
        part = parts[which]
        chunk = part.shape[2]
        rows = value.shape[0]
        for p in range(n):
            lo, hi = max(p * chunk, first), min((p + 1) * chunk, first + rows)
            if lo < hi:
                part[p // half, p % half, lo - p * chunk : hi - p * chunk, :] = value[
                    lo - first : hi - first, :
                ]

    def clear_tail(which, rows):
        part = parts[which]
        for p in range(n):
            if (p + 1) * part.shape[2] > rows:
                part[p // half, p % half] = jnp.zeros(part.shape[2:], F32)

    def unfill(which, first, rows):
        full = fulls[which]
        chunk = full.shape[2]
        pieces = []
        for p in range(n):
            lo, hi = max(p * chunk, first), min((p + 1) * chunk, first + rows)
            if lo < hi:
                pieces.append(full[p // half, p % half, lo - p * chunk : hi - p * chunk, :])
        return jnp.concatenate(pieces, axis=0)

    for which in range(kinds):
        clear_tail(which, 3 * d if which == 0 else d)
    node_input = jnp.concatenate([nf_ref[...], consistent], axis=1)
    fill(0, 0, mm_lt(node_input, node_back))
    fill(0, 2 * d, mm_lt(node_hidden.astype(BF16), cot_n))
    bias_s[2:3, :] = jnp.sum(node_back.astype(F32), axis=0, keepdims=True)
    stage_one(0)
    node_base = node_cot + mm_rt(node_back, wn[:d, :])

    agg_back = take_shared(agg_s[...], in2, copies)
    stage_two(0)
    arrive(15, 16)
    highs, lows = halves(agg_back)
    quad = jnp.concatenate(
        [highs[e * NPE : (e + 1) * NPE, :] for e in range(slots)]
        + [lows[e * NPE : (e + 1) * NPE, :] for e in range(slots)],
        axis=1,
    )

    def backward(c, sums):
        rows = pl.ds(pl.multiple_of(c * ch, 16), ch)
        got = mm(tab_t[rows, :], quad)
        for e in range(slots):
            here = ef_rows(e, c)
            given = jnp.where(
                jnp.broadcast_to(live, (ch, d)) > e, ec_ref[here, :].astype(F32), 0.0
            )
            cot = given + (got[:, e * d : (e + 1) * d] + got[:, (slots + e) * d : (slots + e + 1) * d])
            ecot_s[here, :] = cot
            half = cot.astype(BF16)
            cot_s[here, :] = half
            eb = (mm_rt(half, wo) * slope_s[here, :]).astype(BF16)
            eb_s[here, :] = eb
            sums = (
                sums[0] + jnp.sum(eb.astype(F32), axis=0, keepdims=True),
                sums[1] + jnp.sum(half.astype(F32), axis=0, keepdims=True),
            )
        return sums

    zero = jnp.zeros((1, d), F32)
    sums = lax.fori_loop(0, n_ch, backward, (zero, zero))
    bias_s[0:1, :] = sums[0]
    bias_s[1:2, :] = sums[1]

    def bias_copy(i):
        return pltpu.make_async_remote_copy(
            src_ref=bias_s,
            dst_ref=bias_l.at[i - 1],
            send_sem=bs_send.at[i - 1],
            recv_sem=bs_recv.at[i - 1],
            device_id=device(lax.rem(me + i, n)),
            device_id_type=MESH,
        )

    fill(1, 0, mm_lt(hid_s[...], cot_s[...]))
    stage_one(1)
    stage_three(0)
    lax.fori_loop(1, n, lambda i, x: (bias_copy(i).start(), x)[1], 0)

    fill(2, 0, mm_lt(ef_ref[...], eb_s[...]))
    stage_one(2)
    eb2 = stacked(eb_s)
    unstack = lambda v: jnp.concatenate(
        [v[:, e * d : (e + 1) * d] for e in range(slots)], axis=0
    )
    by_target = jnp.concatenate(halves(unstack(mm(tab_tt[...], eb2))), axis=1)
    grads = mm_lt(nf_ref[...], by_target)
    fill(3, 0, grads[:, :d] + grads[:, d:])
    stage_one(3)
    stage_two(1)
    source_row = ends[0:1, :]
    node_id = lax.broadcasted_iota(jnp.int32, (NPE, edges), 0).astype(F32)
    source_hit = jnp.where(source_row == node_id, 1.0, 0.0).astype(BF16)
    by_source = jnp.concatenate(halves(unstack(mm(source_hit, eb2))), axis=1)
    grads = mm_lt(nf_ref[...], by_source)
    fill(4, 0, grads[:, :d] + grads[:, d:])
    stage_one(4)
    stage_two(2)
    stage_two(3)
    stage_four(0)

    ws, wt = wi[:d, :], wi[d : 2 * d, :]
    w4 = jnp.concatenate([ws, ws, wt, wt], axis=1)
    spread = jnp.concatenate([by_source, by_target], axis=1)
    ng_ref[...] = (node_base + mm_rt(spread, w4)).astype(BF16)
    ng_out = pltpu.make_async_copy(ng_ref, ng_any, out_sem.at[0])
    ng_out.start()
    stage_two(4)
    stage_three(1)
    we = wi[2 * d :, :]

    def last(c, carry):
        rows = pl.ds(pl.multiple_of(c * ch, 16), ch)
        eg_ref[rows, :] = (ecot_s[rows, :] + mm_rt(eb_s[rows, :], we)).astype(BF16)
        return carry

    lax.fori_loop(0, n_ch * slots, last, 0)
    eg_out = pltpu.make_async_copy(eg_ref, eg_any, out_sem.at[1])
    eg_out.start()
    stage_three(2)
    stage_three(3)
    stage_three(4)

    def add_bias(i, total):
        bias_copy(i).wait()
        return total + bias_l[i - 1]

    bias = lax.fori_loop(1, n, add_bias, bias_s[...])
    gbi_ref[...] = bias[0:1, :] * edge_scale
    gbo_ref[...] = bias[1:2, :] * edge_scale
    gbn_ref[...] = bias[2:3, :] * node_scale
    gbq_ref[...] = bias[3:4, :] * node_scale
    for which in range(1, kinds):
        stage_four(which)
    stage_five(0)
    gwn_ref[...] = unfill(0, 0, 2 * d) * node_scale
    gwq_ref[...] = unfill(0, 2 * d, d) * node_scale
    stage_five(1)
    gwo_ref[...] = unfill(1, 0, d) * edge_scale
    ng_out.wait()
    eg_out.wait()
    for which, first in ((2, 2 * d), (3, d), (4, 0)):
        stage_five(which)
        gwi_ref[first : first + d, :] = unfill(which, 0, d) * edge_scale


def deliver(*refs):
    count = len(refs) // 2
    sems = refs[-1]
    copies = [
        pltpu.make_async_copy(refs[i], refs[count + i], sems.at[i]) for i in range(count)
    ]
    for copy in copies:
        copy.start()
    for copy in copies:
        copy.wait()


_axis_order = ("dom", "rep")


def body(
    node_features, edge_features, node_cotangent, edge_cotangent,
    edge_in_weight, edge_in_bias, edge_out_weight, edge_out_bias,
    node_in_weight, node_in_bias, node_out_weight,
    edge_ends, live_elements, shared_nodes, shared_counts, multiplicity,
):
    n = lax.axis_size("dom")
    nodes, d = node_features.shape
    rows = edge_features.shape[0]
    edges = edge_ends.shape[1]
    s_count = shared_nodes.shape[2]
    hid = edge_in_weight.shape[1]
    edge_scale = 1.0 / math.sqrt(rows * n)
    node_scale = 1.0 / math.sqrt(nodes * n)
    chunk = lambda total: -(-total // (8 * n)) * 8
    chunks = [chunk(3 * d)] + [chunk(d)] * 4
    half = n // 2
    vmem = pl.BlockSpec(memory_space=pltpu.VMEM)
    raw = pl.BlockSpec(memory_space=pl.ANY)
    hbm = pl.BlockSpec(memory_space=pltpu.HBM)
    shape = jax.ShapeDtypeStruct
    dma = pltpu.SemaphoreType.DMA
    row = shape((1, d), F32)
    args = (
        node_features, edge_features, node_cotangent, edge_cotangent,
        edge_in_weight, edge_in_bias.reshape(1, -1), edge_out_weight, edge_out_bias.reshape(1, -1),
        node_in_weight, node_in_bias.reshape(1, -1), node_out_weight,
        edge_ends, live_elements.reshape(1, 1), shared_nodes[0], shared_counts,
        multiplicity.reshape(-1, LANES),
    )
    outs = pl.pallas_call(
        functools.partial(fused, n, n // 4, edge_scale, node_scale),
        out_shape=(
            shape((nodes, d), BF16), shape((rows, d), BF16),
            shape((3 * d, hid), F32), row, shape((hid, d), F32), row,
            shape((2 * d, hid), F32), row, shape((hid, d), F32), row,
        ),
        in_specs=[hbm] * len(args),
        out_specs=(hbm,) * 2 + (vmem,) * 8,
        scratch_shapes=[
            pltpu.VMEM((edges, LANES), F32), pltpu.VMEM((edges, LANES), F32),
            pltpu.VMEM((edges, NPE), BF16), pltpu.VMEM((NPE, edges), BF16),
            pltpu.VMEM((4 * s_count, nodes), BF16), pltpu.VMEM((nodes, 4 * s_count), BF16),
            pltpu.VMEM((rows, hid), F32), pltpu.VMEM((rows, hid), BF16),
            pltpu.VMEM((rows, hid), BF16), pltpu.VMEM((rows, d), BF16), pltpu.VMEM((rows, d), F32),
            pltpu.VMEM((nodes, d), F32), pltpu.VMEM((nodes, d), F32),
        ]
        + [pltpu.VMEM((4, s_count, d), F32)] * 4
        + [pltpu.VMEM(arg.shape, arg.dtype) for arg in args]
        + [dma((len(args),)), pltpu.VMEM((nodes, d), BF16), pltpu.VMEM((rows, d), BF16), dma((2,))]
        + [pltpu.VMEM((8, d), F32), pltpu.VMEM((n - 1, 8, d), F32)]
        + [dma((2, 4)), dma((2, 4))]
        + [dma((2, len(chunks)))] * 2
        + [dma((len(chunks), half - 1))] * 4
        + [dma((n - 1,))] * 2
        + [pltpu.VMEM((2, half, c, d), F32) for c in chunks]
        + [pltpu.VMEM((half, c, d), F32) for c in chunks]
        + [pltpu.VMEM((half - 1, c, d), F32) for c in chunks]
        + [pltpu.VMEM((2, half, c, d), F32) for c in chunks],
        compiler_params=pltpu.CompilerParams(
            collective_id=0, has_side_effects=True, vmem_limit_bytes=60 << 20
        ),
    )(*args)
    outs = pl.pallas_call(
        deliver,
        out_shape=tuple(shape(out.shape, out.dtype) for out in outs),
        in_specs=[vmem] * len(outs),
        out_specs=(raw,) * len(outs),
        scratch_shapes=[dma((len(outs),))],
        compiler_params=pltpu.CompilerParams(vmem_limit_bytes=60 << 20),
    )(*outs)
    flat = lambda v: v.reshape(-1)
    return (
        outs[0], outs[1], outs[2], flat(outs[3]), outs[4], flat(outs[5]),
        outs[6], flat(outs[7]), outs[8], flat(outs[9]),
    )


def solution(mesh):
    global _axis_order
    _axis_order = tuple(mesh.axis_names)
    both = P(("rep", "dom"))
    both2 = P(("rep", "dom"), None)
    in_specs = (
        (both2,) * 4 + (P(),) * 8 + (both, P(("rep", "dom"), None, None), both2, both)
    )
    out_specs = (both2, both2) + (P("rep", None), P("rep")) * 4
    return jax.shard_map(body, mesh=mesh, in_specs=in_specs, out_specs=out_specs, check_vma=False)
```

profile of v0, /device:TPU:0, one launch (start us, length us, event | category | flops | bytes accessed | tf_op | source)
XLA Modules:
  0.0 47.1 jit_solution(11333114637959649753)
XLA Ops:
  1.3 43.3 %shard_map.231 = (bf16[1024,128]{1,0:T(8,128)(2,1)}, bf16[2688,128]{1,0:T(8,128)(2,1)}, f32[384,128]{1,0:T(8,128)}, f32[1,128]{1,0:T(1,128)}, f32[128,128]{1,0:T...) custom-call(bf16[1024,128]{1,0:T(8,128)(2,1)} %nf_any.1, ...), custom_call_target="tpu_custom_call" | custom-call | tf_op jit(solution)/shard_map/pallas_call | solution.py:510
  44.6 2.5 %shard_map.232 = (bf16[1024,128]{1,0:T(8,128)(2,1)}, bf16[2688,128]{1,0:T(8,128)(2,1)}, f32[384,128]{1,0:T(8,128)}, f32[1,128]{1,0:T(1,128)}, f32[128,128]{1,0:T...) custom-call(bf16[1024,128]{1,0:T(8,128)(2,1)} %get-tuple-element.30., ...), custom_call_target="tpu_custom_call" | custom-call | tf_op jit(solution)/shard_map/pallas_call | solution.py:543
where the time goes:
time: 47.3 us; the launch traced here: 47.1 us
  Pallas kernels  45.8 us (97%)
  between operations  1.3 us (3%)
    pallas_call x1, Pallas kernels, body(): pl.pallas_call(functools.partial(fused, n, n // 4, edge_scale, node_scale...  43.3 us
    pallas_call x1, Pallas kernels, body(): pl.pallas_call(deliver, out_shape=tuple((shape(out.shape, out.dtype) for...  2.48 us

commit v1 on v0

--- a/solution.py
+++ b/solution.py
@@ -63,11 +63,11 @@
     n, quarter, edge_scale, node_scale,
     nf_any, ef_any, nc_any, ec_any, wi_any, bi_any, wo_any, bo_any, wn_any, bn_any, wq_any,
     ends_any, live_any, lists_any, counts_any, mult_any,
-    ng_any, eg_any, gwi_ref, gbi_ref, gwo_ref, gbo_ref, gwn_ref, gbn_ref, gwq_ref, gbq_ref,
+    ng_ref, eg_ref, gwi_ref, gbi_ref, gwo_ref, gbo_ref, gwn_ref, gbn_ref, gwq_ref, gbq_ref,
     col_s, col_t, tab_t, tab_tt, pick, pick_t, slope_s, hid_s, eb_s, cot_s, ecot_s,
     inv_s, agg_s, out1, in1, out2, in2,
     nf_ref, ef_ref, nc_ref, ec_ref, wi_ref, bi_ref, wo_ref, bo_ref, wn_ref, bn_ref, wq_ref,
-    ends_ref, live_ref, lists_ref, counts_ref, mult_ref, in_sem, ng_ref, eg_ref, out_sem, bias_s, bias_l,
+    ends_ref, lists_ref, counts_ref, mult_ref, in_sem, out_sem, bias_s, bias_l,
     px_send, px_recv, pair_send, pair_recv, rs_send, rs_recv, ag_send, ag_recv, bs_send, bs_recv,
     *buffers,
 ):
@@ -91,11 +91,11 @@
     parts, pair_land, lands, fulls = (buffers[i * kinds : (i + 1) * kinds] for i in range(4))
     sources = (
         ends_any, nf_any, wi_any, bi_any, ef_any, wo_any, bo_any, counts_any, lists_any,
-        mult_any, live_any, wq_any, wn_any, bn_any, nc_any, ec_any,
+        mult_any, wq_any, wn_any, bn_any, nc_any, ec_any,
     )
     targets = (
         ends_ref, nf_ref, wi_ref, bi_ref, ef_ref, wo_ref, bo_ref, counts_ref, lists_ref,
-        mult_ref, live_ref, wq_ref, wn_ref, bn_ref, nc_ref, ec_ref,
+        mult_ref, wq_ref, wn_ref, bn_ref, nc_ref, ec_ref,
     )
     loads = [
         pltpu.make_async_copy(source, target, in_sem.at[i])
@@ -214,11 +214,11 @@
         pick_t[:, k * s_count : (k + 1) * s_count] = jnp.where(
             lists[k] == node_id, 1.0, 0.0
         ).astype(BF16)
-    arrive(9, 15)
+    arrive(9, 14)
     mult = mult_ref[...].astype(F32)
     for b in range(nodes // LANES):
         inv_s[b * LANES : (b + 1) * LANES, :] = 1.0 / columns_of(mult[b : b + 1, :])
-    live = live_ref[...]
+    live = live_any[0]
     slot_of = lax.broadcasted_iota(jnp.int32, (nodes, d), 0) // NPE
     node_cot = jnp.where(slot_of < live, nc_ref[...].astype(F32), 0.0)
     cot_n = node_cot.astype(BF16)
@@ -347,7 +347,7 @@
 
     agg_back = take_shared(agg_s[...], in2, copies)
     stage_two(0)
-    arrive(15, 16)
+    arrive(14, 15)
     highs, lows = halves(agg_back)
     quad = jnp.concatenate(
         [highs[e * NPE : (e + 1) * NPE, :] for e in range(slots)]
@@ -421,8 +421,6 @@
     w4 = jnp.concatenate([ws, ws, wt, wt], axis=1)
     spread = jnp.concatenate([by_source, by_target], axis=1)
     ng_ref[...] = (node_base + mm_rt(spread, w4)).astype(BF16)
-    ng_out = pltpu.make_async_copy(ng_ref, ng_any, out_sem.at[0])
-    ng_out.start()
     stage_two(4)
     stage_three(1)
     we = wi[2 * d :, :]
@@ -433,8 +431,6 @@
         return carry
 
     lax.fori_loop(0, n_ch * slots, last, 0)
-    eg_out = pltpu.make_async_copy(eg_ref, eg_any, out_sem.at[1])
-    eg_out.start()
     stage_three(2)
     stage_three(3)
     stage_three(4)
@@ -455,8 +451,6 @@
     gwq_ref[...] = unfill(0, 2 * d, d) * node_scale
     stage_five(1)
     gwo_ref[...] = unfill(1, 0, d) * edge_scale
-    ng_out.wait()
-    eg_out.wait()
     for which, first in ((2, 2 * d), (3, d), (4, 0)):
         stage_five(which)
         gwi_ref[first : first + d, :] = unfill(which, 0, d) * edge_scale
@@ -499,23 +493,25 @@
     hbm = pl.BlockSpec(memory_space=pltpu.HBM)
     shape = jax.ShapeDtypeStruct
     dma = pltpu.SemaphoreType.DMA
-    row = shape((1, d), F32)
+    vshape = pltpu.VMEM
+    row = vshape((1, d), F32)
     args = (
         node_features, edge_features, node_cotangent, edge_cotangent,
         edge_in_weight, edge_in_bias.reshape(1, -1), edge_out_weight, edge_out_bias.reshape(1, -1),
         node_in_weight, node_in_bias.reshape(1, -1), node_out_weight,
-        edge_ends, live_elements.reshape(1, 1), shared_nodes[0], shared_counts,
+        edge_ends, live_elements, shared_nodes[0], shared_counts,
         multiplicity.reshape(-1, LANES),
     )
+
     outs = pl.pallas_call(
         functools.partial(fused, n, n // 4, edge_scale, node_scale),
         out_shape=(
-            shape((nodes, d), BF16), shape((rows, d), BF16),
-            shape((3 * d, hid), F32), row, shape((hid, d), F32), row,
-            shape((2 * d, hid), F32), row, shape((hid, d), F32), row,
+            vshape((nodes, d), BF16), vshape((rows, d), BF16),
+            vshape((3 * d, hid), F32), row, vshape((hid, d), F32), row,
+            vshape((2 * d, hid), F32), row, vshape((hid, d), F32), row,
         ),
-        in_specs=[hbm] * len(args),
-        out_specs=(hbm,) * 2 + (vmem,) * 8,
+        in_specs=[hbm] * 12 + [pl.BlockSpec(memory_space=pltpu.SMEM)] + [hbm] * 3,
+        out_specs=(vmem,) * 10,
         scratch_shapes=[
             pltpu.VMEM((edges, LANES), F32), pltpu.VMEM((edges, LANES), F32),
             pltpu.VMEM((edges, NPE), BF16), pltpu.VMEM((NPE, edges), BF16),
@@ -525,8 +521,8 @@
             pltpu.VMEM((nodes, d), F32), pltpu.VMEM((nodes, d), F32),
         ]
         + [pltpu.VMEM((4, s_count, d), F32)] * 4
-        + [pltpu.VMEM(arg.shape, arg.dtype) for arg in args]
-        + [dma((len(args),)), pltpu.VMEM((nodes, d), BF16), pltpu.VMEM((rows, d), BF16), dma((2,))]
+        + [pltpu.VMEM(arg.shape, arg.dtype) for i, arg in enumerate(args) if i != 12]
+        + [dma((len(args),)), dma((2,))]
         + [pltpu.VMEM((8, d), F32), pltpu.VMEM((n - 1, 8, d), F32)]
         + [dma((2, 4)), dma((2, 4))]
         + [dma((2, len(chunks)))] * 2
@@ -546,7 +542,7 @@
         in_specs=[vmem] * len(outs),
         out_specs=(raw,) * len(outs),
         scratch_shapes=[dma((len(outs),))],
-        compiler_params=pltpu.CompilerParams(vmem_limit_bytes=60 << 20),
+        compiler_params=pltpu.CompilerParams(vmem_limit_bytes=8 << 20),
     )(*outs)
     flat = lambda v: v.reshape(-1)
     return (

time: 47.3 us -> 45.3 us (0.958)
  Pallas kernels: 45.8 us -> 43.7 us
    pallas_call x1, Pallas kernels: 2.48 us -> 1.18 us  [body(): pl.pallas_call(deliver, out_shape=tuple((shape(out.shape, out.dtype) for...]
    pallas_call x1, Pallas kernels: 43.3 us -> 42.5 us  [body(): pl.pallas_call(functools.partial(fused, n, n // 4, edge_scale, node_scale...]
where the time goes in v1:
time: 45.3 us; the launch traced here: 45 us
  Pallas kernels  43.7 us (96%)
  between operations  1.3 us (3%)
    pallas_call x1, Pallas kernels, body(): pl.pallas_call(functools.partial(fused, n, n // 4, edge_scale, node_scale...  42.5 us
    pallas_call x1, Pallas kernels, body(): pl.pallas_call(deliver, out_shape=tuple((shape(out.shape, out.dtype) for...  1.18 us

profile of v1, /device:TPU:0, one launch (start us, length us, event | category | flops | bytes accessed | tf_op | source)
XLA Modules:
  0.0 45.0 jit_solution(17519644368393121865)
XLA Ops:
  1.3 42.5 %shard_map.231 = (bf16[1024,128]{1,0:T(8,128)(2,1)S(1)}, bf16[2688,128]{1,0:T(8,128)(2,1)S(1)}, f32[384,128]{1,0:T(8,128)S(1)}, f32[1,128]{1,0:T(1,128)S(1)}, f3...) custom-call(bf16[1024,128]{1,0:T(8,128)(2,1)} %nf_any.1, ...), custom_call_target="tpu_custom_call" | custom-call | tf_op jit(solution)/shard_map/pallas_call | solution.py:506
  43.8 1.2 %shard_map.232 = (bf16[1024,128]{1,0:T(8,128)(2,1)}, bf16[2688,128]{1,0:T(8,128)(2,1)}, f32[384,128]{1,0:T(8,128)}, f32[1,128]{1,0:T(1,128)}, f32[128,128]{1,0:T...) custom-call(bf16[1024,128]{1,0:T(8,128)(2,1)S(1)} %get-tuple-element, ...), custom_call_target="tpu_custom_call" | custom-call | tf_op jit(solution)/shard_map/pallas_call | solution.py:539

commit v2 on v1

v2 whole, which is shorter than its diff:
```python
import functools
import math

import jax
import jax.numpy as jnp
from jax import lax
from jax.experimental import pallas as pl
from jax.experimental.pallas import tpu as pltpu
from jax.sharding import PartitionSpec as P

NPE = 512
LANES = 128
F32 = jnp.float32
BF16 = jnp.bfloat16
MESH = pl.DeviceIdType.MESH
CHUNK = 448


def divisor_up_to(total, cap):
    best = 16
    for size in range(16, cap + 1, 16):
        if total % size == 0:
            best = size
    return best


def mm(left, right):
    return lax.dot_general(left, right, (((1,), (0,)), ((), ())), preferred_element_type=F32)


def half_of(rows):
    return rows // 32 * 16


def in_two(step, left, right):
    cut = half_of(left.shape[0])
    return jnp.concatenate([step(left[:cut, :], right), step(left[cut:, :], right)], axis=0)


def mm2(left, right):
    return in_two(mm, left, right)


def mm_rt2(left, right):
    return in_two(mm_rt, left, right)


def mm_lt2(left, right):
    cut = half_of(left.shape[0])
    return mm_lt(left[:cut, :], right[:cut, :]) + mm_lt(left[cut:, :], right[cut:, :])


def mm_rt(left, right):
    return lax.dot_general(left, right, (((1,), (1,)), ((), ())), preferred_element_type=F32)


def mm_lt(left, right):
    return lax.dot_general(left, right, (((0,), (0,)), ((), ())), preferred_element_type=F32)


def halves(value):
    high = value.astype(BF16)
    low = (value - high.astype(F32)).astype(BF16)
    return high, low


def columns_of(row):
    return jnp.transpose(jnp.broadcast_to(row, (LANES, row.shape[1])))


def hits(ids, width, shift=0):
    lane = lax.broadcasted_iota(jnp.int32, ids.shape, 1).astype(F32)
    moved = ids + float(shift) if shift else ids
    tiles = [
        jnp.where(moved == lane + float(LANES * t + shift), 1.0, 0.0).astype(BF16)
        for t in range(width // LANES)
    ]
    return jnp.concatenate(tiles, axis=1)


def row_hits(row, height, shift=0):
    node = (lax.broadcasted_iota(jnp.int32, (height, row.shape[1]), 0) + shift).astype(F32)
    return jnp.where(row + float(shift) == node, 1.0, 0.0).astype(BF16)


def repeated(weight, times):
    rows, cols = weight.shape
    zero = jnp.zeros((rows, cols), weight.dtype)
    return jnp.concatenate(
        [
            jnp.concatenate([weight if a == b else zero for b in range(times)], axis=1)
            for a in range(times)
        ],
        axis=0,
    )


def activation(linear):
    squashed = 0.5 * jnp.tanh(0.5 * linear) + 0.5
    return linear * squashed, squashed * (1.0 + linear * (1.0 - squashed))


def fused(
    n, quarter, edge_scale, node_scale,
    nf_any, ef_any, nc_any, ec_any, wi_any, bi_any, wo_any, bo_any, wn_any, bn_any, wq_any,
    ends_any, live_any, lists_any, counts_any, mult_any,
    ng_ref, eg_ref, gwi_ref, gbi_ref, gwo_ref, gbo_ref, gwn_ref, gbn_ref, gwq_ref, gbq_ref,
    col_s, col_t, lcol, rows_s, deg_s, src_s, tgt_s, hid_s, slope_s, lin_s, giv_s, join_t, eb_s,
    sum_s, sum_t, pick_t, gwo_s, cot_s, hback_s, early_s, base_s, inv_s, agg_s,
    out1, in1, out2, in2,
    nf_ref, ef_ref, nc_ref, ec_ref, wi_ref, bi_ref, wo_ref, bo_ref, wn_ref, bn_ref, wq_ref,
    ends_ref, lists_ref, counts_ref, mult_ref, in_sem, bias_s, bias_l,
    px_send, px_recv, bs_send, bs_recv,
    qparts, qlands, mids, clands, qs_send, qs_recv, cs_send, cs_recv, gs_send, gs_recv,
):
    nodes = nf_ref.shape[0]
    d = nf_ref.shape[1]
    slots = nodes // NPE
    wide = slots * d
    edges = ends_ref.shape[1]
    me = lax.axis_index("dom")
    rep = lax.axis_index("rep")
    offsets = (1, -1, quarter, -quarter)
    order = _axis_order
    ch = divisor_up_to(edges, CHUNK)
    n_ch = edges // ch

    def device(index):
        return tuple(index if name == "dom" else rep for name in order)

    team, seat = me // 4, lax.rem(me, 4)
    teams = n // 4
    groups = (
        ((ends_any, ends_ref),),
        ((nf_any, nf_ref), (wi_any, wi_ref), (bi_any, bi_ref), (ef_any, ef_ref)),
        ((lists_any, lists_ref), (counts_any, counts_ref)),
        ((wo_any, wo_ref), (bo_any, bo_ref)),
        (
            (mult_any, mult_ref), (wq_any, wq_ref), (wn_any, wn_ref), (bn_any, bn_ref),
            (nc_any, nc_ref), (ec_any, ec_ref),
        ),
    )
    loads = []
    count = 0
    for group in groups:
        loads.append([])
        for source, target in group:
            loads[-1].append(pltpu.make_async_copy(source, target, in_sem.at[count]))
            loads[-1][-1].start()
            count += 1

    def arrive(which):
        for load in loads[which]:
            load.wait()

    barrier = pltpu.get_barrier_semaphore()

    def greet(i, carry):
        pl.semaphore_signal(
            barrier, inc=1, device_id=device(lax.rem(me + i, n)), device_id_type=MESH
        )
        return carry

    lax.fori_loop(1, n, greet, 0)

    arrive(0)
    ends = ends_ref[...].astype(F32)
    source_row, target_row = ends[0:1, :], ends[1:2, :]
    for start in range(0, edges, LANES):
        stop = min(start + LANES, edges)
        col_t[start:stop, :] = columns_of(ends[1:2, start:stop])
        col_s[start:stop, :] = columns_of(ends[0:1, start:stop])
    arrive(1)
    wi = wi_ref[...]
    ws, wt, we = wi[:d, :], wi[d : 2 * d, :], wi[2 * d :, :]
    by_slot = lambda v: jnp.concatenate(
        [v[e * NPE : (e + 1) * NPE, :] for e in range(slots)], axis=1
    )
    by_row = lambda v: jnp.concatenate(
        [v[:, e * d : (e + 1) * d] for e in range(slots)], axis=0
    )
    fold = lambda v: v[:, :d] + v[:, d:]
    pair_of = lambda v: jnp.concatenate(halves(v), axis=1)
    across = lambda ref, first, count, step: jnp.concatenate(
        [ref[e * step + first : e * step + first + count, :] for e in range(slots)], axis=1
    )
    twice = lambda v: jnp.concatenate([v] * slots, axis=1)
    nf2 = by_slot(nf_ref[...])
    w_in = jnp.concatenate([repeated(w, slots) for w in (ws, wt, we)], axis=0)
    bi_wide = twice(bi_ref[...])

    for c in range(n_ch):
        rows = slice(c * ch, (c + 1) * ch)
        target = mm(hits(col_t[rows, :], NPE), nf2).astype(BF16)
        source = mm(hits(col_s[rows, :], NPE), nf2).astype(BF16)
        src_s[rows, :] = source
        tgt_s[rows, :] = target
        joined = jnp.concatenate([source, target, across(ef_ref, c * ch, ch, edges)], axis=1)
        hidden, slope = activation(mm2(joined, w_in) + bi_wide)
        hid_s[rows, :] = hidden.astype(BF16)
        slope_s[rows, :] = slope

    arrive(2)
    s_count = lists_ref.shape[1]
    lane_row = lax.broadcasted_iota(jnp.int32, (1, s_count), 1)
    for k in range(4):
        row = jnp.where(
            lane_row < counts_ref[:, k : k + 1], lists_ref[k : k + 1, :], -1
        ).astype(F32)
        rows_s[k] = jnp.broadcast_to(row, (8, s_count))
        lcol[k * s_count : (k + 1) * s_count, :] = columns_of(row)
    arrive(3)
    wo = wo_ref[...]
    wo_wide = repeated(wo, slots)
    nb = 128
    for b in range(NPE // nb):
        node_id = (lax.broadcasted_iota(jnp.int32, (nb, edges), 0) + b * nb).astype(F32)
        deg_s[b * nb : (b + 1) * nb, :] = jnp.broadcast_to(
            jnp.sum(jnp.where(target_row == node_id, 1.0, 0.0), axis=1, keepdims=True), (nb, d)
        )
    sums = mm(
        row_hits(target_row, NPE),
        jnp.concatenate([across(ef_ref, 0, edges, edges), hid_s[...]], axis=1),
    )
    sum_s[...] = sums[:, wide:]
    agg2 = (
        sums[:, :wide]
        + mm2(pair_of(sums[:, wide:]), jnp.concatenate([wo_wide, wo_wide], axis=0))
        + twice(deg_s[...] * bo_ref[...])
    )
    agg_s[...] = by_row(agg2)

    upper = me >= n // 2
    turns = [jnp.where(upper, a, b) for a, b in ((2, 3), (0, 1), (3, 2), (1, 0))]
    steps = [jnp.where(upper, offsets[a], offsets[b]) for a, b in ((2, 3), (0, 1), (3, 2), (1, 0))]

    def partner_copy(out, incoming, which, j):
        k = turns[j]
        other = k + 1 - 2 * lax.rem(k, 2)
        return pltpu.make_async_remote_copy(
            src_ref=out.at[k],
            dst_ref=incoming.at[other],
            send_sem=px_send.at[which],
            recv_sem=px_recv.at[which, other],
            device_id=device(lax.rem(me + steps[j] + n, n)),
            device_id_type=MESH,
        )

    def landing(out, incoming, which, j):
        k = turns[j]
        return pltpu.make_async_remote_copy(
            src_ref=out.at[k],
            dst_ref=incoming.at[k],
            send_sem=px_send.at[which],
            recv_sem=px_recv.at[which, k],
            device_id=device(lax.rem(me + 1, n)),
            device_id_type=MESH,
        )

    def send_shared(values, out, incoming, which):
        pair = pair_of(values)
        for k in range(4):
            out[k] = fold(
                mm(hits(lcol[k * s_count : (k + 1) * s_count, :], nodes, which), pair)
            )
        for j in range(4):
            partner_copy(out, incoming, which, j).start()

    def landed(out, incoming, which, js):
        for j in js:
            landing(out, incoming, which, j).wait_recv()
        moved = jnp.concatenate([incoming[turns[j]] for j in js], axis=0)
        entries = jnp.concatenate([rows_s[turns[j]][0:1, :] for j in js], axis=1)
        return pair_of(moved), entries

    near, far = (2, 3), (0, 1)
    pl.semaphore_wait(barrier, n - 1)
    send_shared(agg_s[...], out1, in1, 0)

    arrive(4)
    mult = mult_ref[...].astype(F32)
    for b in range(nodes // LANES):
        inv_s[b * LANES : (b + 1) * LANES, :] = 1.0 / columns_of(mult[b : b + 1, :])
    live = live_any[0]
    slot_of = lax.broadcasted_iota(jnp.int32, (nodes, d), 0) // NPE
    node_cot = jnp.where(slot_of < live, nc_ref[...].astype(F32), 0.0)
    cot_s[...] = node_cot.astype(BF16)
    wn = wn_ref[...]
    wn_wide = repeated(wn[d:, :], slots)
    hback_s[...] = mm_rt2(by_slot(cot_s[...]), repeated(wq_ref[...], slots))
    early_s[...] = mm2(nf2, repeated(wn[:d, :], slots)) + twice(bn_ref[...])
    bias_s[...] = jnp.zeros_like(bias_s)
    bias_s[3:4, :] = jnp.sum(node_cot, axis=0, keepdims=True)

    given_sum = jnp.zeros((1, d), F32)
    gwo = jnp.zeros((d, d), F32)
    for e in range(slots):
        lanes = slice(e * d, (e + 1) * d)
        given = jnp.where(
            jnp.broadcast_to(live, (edges, d)) > e,
            ec_ref[e * edges : (e + 1) * edges, :].astype(F32),
            0.0,
        )
        given_sum = given_sum + jnp.sum(given, axis=0, keepdims=True)
        giv_s[:, lanes] = given.astype(BF16)
        gwo = gwo + mm_lt(hid_s[:, lanes], giv_s[:, lanes])
    gwo_s[...] = gwo
    lin_s[...] = mm_rt2(giv_s[...], wo_wide)
    for at, block in enumerate((src_s[...], tgt_s[...], across(ef_ref, 0, edges, edges))):
        join_t[at * wide : (at + 1) * wide, :] = jnp.transpose(block)
    sum_rows = pair_of(by_row(sum_s[...]))
    picked = fold(mm2(hits(lcol[...], nodes, 2), sum_rows))
    pick_t[...] = jnp.transpose(pair_of(picked))
    sum_t[...] = jnp.transpose(sum_rows)

    def gather_in(js):
        moved, entries = landed(out1, in1, 0, js)
        return agg_s[...] + fold(mm2(row_hits(entries, nodes), moved))

    agg_s[...] = gather_in(near)
    consistent = (gather_in(far) * inv_s[...]).astype(BF16)
    node_hidden, node_slope = activation(early_s[...] + mm2(by_slot(consistent), wn_wide))
    node_back2 = (hback_s[...] * node_slope).astype(BF16)
    back = by_row(mm_rt2(node_back2, wn_wide)) * inv_s[...]
    agg_s[...] = back
    send_shared(back, out2, in2, 1)

    quart = qparts.shape[2]
    results = (
        (gwn_ref, 0, node_scale), (gwn_ref, d, node_scale), (gwq_ref, 0, node_scale),
        (gwo_ref, 0, edge_scale),
        (gwi_ref, 2 * d, edge_scale), (gwi_ref, d, edge_scale), (gwi_ref, 0, edge_scale),
    )

    def seat_of(i):
        return lax.rem(seat + i, 4)

    def split_copy(p, i):
        return pltpu.make_async_remote_copy(
            src_ref=qparts.at[p, seat_of(i)],
            dst_ref=qlands.at[p, i - 1],
            send_sem=qs_send,
            recv_sem=qs_recv.at[p],
            device_id=device(4 * team + seat_of(i)),
            device_id_type=MESH,
        )

    def cross_copy(p, i):
        return pltpu.make_async_remote_copy(
            src_ref=mids.at[p],
            dst_ref=clands.at[p, i - 1],
            send_sem=cs_send,
            recv_sem=cs_recv.at[p],
            device_id=device(4 * lax.rem(team + i, teams) + seat),
            device_id_type=MESH,
        )

    def share_copy(p, i):
        ref, first, _ = results[p]
        rows = pl.ds(pl.multiple_of(first + seat * quart, 8), quart)
        return pltpu.make_async_remote_copy(
            src_ref=ref.at[rows],
            dst_ref=ref.at[rows],
            send_sem=gs_send,
            recv_sem=gs_recv,
            device_id=device(4 * team + seat_of(i)),
            device_id_type=MESH,
        )

    def whole(ref, send_sem, recv_sem):
        return pltpu.make_async_remote_copy(
            src_ref=ref,
            dst_ref=ref,
            send_sem=send_sem,
            recv_sem=recv_sem,
            device_id=device(lax.rem(me + 1, n)),
            device_id_type=MESH,
        )

    def hold(p, value):
        for j in range(4):
            qparts[p, j] = value[j * quart : (j + 1) * quart, :]

    def push(p):
        for i in (2, 1, 3):
            split_copy(p, i).start()

    def cross(p):
        whole(qlands.at[p], qs_send, qs_recv.at[p]).wait_recv()
        total = qparts[p, seat]
        for i in range(3):
            total = total + qlands[p, i]
        mids[p] = total
        for i in range(1, teams):
            cross_copy(p, i).start()

    def share(p):
        whole(clands.at[p], cs_send, cs_recv.at[p]).wait_recv()
        total = mids[p]
        for i in range(teams - 1):
            total = total + clands[p, i]
        ref, first, scale = results[p]
        ref[pl.ds(pl.multiple_of(first + seat * quart, 8), quart), :] = total * scale
        for i in (2, 1, 3):
            share_copy(p, i).start()

    node_back = by_row(node_back2)
    hold(0, mm_lt2(nf_ref[...], node_back))
    hold(1, mm_lt2(consistent, node_back))
    hold(2, mm_lt2(by_row(node_hidden.astype(BF16)), cot_s[...]))
    bias_s[2:3, :] = jnp.sum(node_back.astype(F32), axis=0, keepdims=True)
    base_s[...] = cot_s[...].astype(F32) + mm_rt2(node_back, wn[:d, :])
    wo_rows = jnp.concatenate([wo, wo], axis=1)
    pair_back = pair_of(back)
    crossed = mm2(sum_t[...], pair_back)
    gwo_s[...] = gwo_s[...] + fold(crossed[:d, :]) + fold(crossed[d:, :])
    spread_back = by_slot(mm_rt2(pair_back, wo_rows))
    for c in range(n_ch):
        rows = slice(c * ch, (c + 1) * ch)
        got = mm(hits(col_t[rows, :], NPE, 1), pair_of(spread_back))
        lin_s[rows, :] = lin_s[rows, :] + got[:, :wide] + got[:, wide:]

    for p in range(3):
        push(p)

    def toward(moved, entries, e):
        wanted = entries - float(NPE * e)
        marks = jnp.concatenate(
            [
                jnp.where(col_t[...] == wanted[:, t * LANES : (t + 1) * LANES], 1.0, 0.0).astype(BF16)
                for t in range(entries.shape[1] // LANES)
            ],
            axis=1,
        )
        return fold(mm(marks, moved))

    moved, entries = landed(out2, in2, 1, near)
    moved = pair_of(mm_rt2(moved, wo_rows))
    for e in range(slots):
        lanes = slice(e * d, (e + 1) * d)
        lin_s[:, lanes] = lin_s[:, lanes] + toward(moved, entries, e)
    moved, entries = landed(out2, in2, 1, far)
    moved = pair_of(mm_rt2(moved, wo_rows))
    for e in range(slots):
        lanes = slice(e * d, (e + 1) * d)
        eb_s[:, lanes] = (
            (lin_s[:, lanes] + toward(moved, entries, e)) * slope_s[:, lanes]
        ).astype(BF16)
    arrived = pair_of(jnp.concatenate([in2[k] for k in range(4)], axis=0))
    added = mm2(pick_t[...], arrived)
    hold(3, gwo_s[...] + fold(added[:d, :]) + fold(added[d:, :]))
    push(3)

    def weigh(at):
        total = None
        for e in range(slots):
            first = at * wide + e * d
            both = mm(join_t[first : first + d, :], eb_s[...])[:, e * d : (e + 1) * d]
            total = both if total is None else total + both
        return total

    for at in (2, 1, 0):
        hold(6 - at, weigh(at))
        push(6 - at)
    column = jnp.sum(eb_s[...].astype(F32), axis=0, keepdims=True)
    bias_row = column[:, :d]
    for e in range(1, slots):
        bias_row = bias_row + column[:, e * d : (e + 1) * d]
    bias_s[0:1, :] = bias_row
    entry_row = jnp.concatenate([rows_s[k][0:1, :] for k in range(4)], axis=1)
    agg_back = agg_s[...] + fold(mm2(row_hits(entry_row, nodes, 1), arrived))
    degrees = jnp.concatenate([deg_s[...]] * slots, axis=0)
    bias_s[1:2, :] = given_sum + jnp.sum(degrees * agg_back, axis=0, keepdims=True)

    def bias_copy(i):
        return pltpu.make_async_remote_copy(
            src_ref=bias_s,
            dst_ref=bias_l.at[i - 1],
            send_sem=bs_send,
            recv_sem=bs_recv,
            device_id=device(lax.rem(me + i, n)),
            device_id_type=MESH,
        )

    lax.fori_loop(1, n, lambda i, x: (bias_copy(i).start(), x)[1], 0)

    eb2 = eb_s[...]
    we_wide = repeated(we, slots)
    quad = pair_of(by_slot(agg_back))
    for c in range(n_ch):
        rows = slice(c * ch, (c + 1) * ch)
        got = mm(hits(col_t[rows, :], NPE, 2), quad)
        cot = giv_s[rows, :].astype(F32) + (got[:, :wide] + got[:, wide:])
        value = (cot + mm_rt(eb_s[rows, :], we_wide)).astype(BF16)
        for e in range(slots):
            eg_ref[e * edges + c * ch : e * edges + (c + 1) * ch, :] = value[
                :, e * d : (e + 1) * d
            ]
    for p in range(0, 4):
        cross(p)
    by_target = pair_of(by_row(mm2(row_hits(target_row, NPE, 1), eb2)))
    for p in range(4, 7):
        cross(p)
    by_source = pair_of(by_row(mm2(row_hits(source_row, NPE, 1), eb2)))
    w4 = jnp.concatenate([ws, ws, wt, wt], axis=1)
    spread = jnp.concatenate([by_source, by_target], axis=1)
    ng_ref[...] = (base_s[...] + mm_rt2(spread, w4)).astype(BF16)
    for p in range(7):
        share(p)

    whole(bias_l, bs_send, bs_recv).wait_recv()
    bias = lax.fori_loop(1, n, lambda i, total: total + bias_l[i - 1], bias_s[...])
    gbi_ref[...] = bias[0:1, :] * edge_scale
    gbo_ref[...] = bias[1:2, :] * edge_scale
    gbn_ref[...] = bias[2:3, :] * node_scale
    gbq_ref[...] = bias[3:4, :] * node_scale
    whole(bias_l, bs_send, bs_recv).wait_send()
    whole(in1, px_send.at[0], px_recv.at[0, 0]).wait_send()
    whole(in2, px_send.at[1], px_recv.at[1, 0]).wait_send()
    whole(qlands, qs_send, qs_recv.at[0]).wait_send()
    whole(clands, cs_send, cs_recv.at[0]).wait_send()
    whole(qlands, gs_send, gs_recv).wait()


def deliver(*refs):
    count = len(refs) // 2
    sems = refs[-1]
    copies = [
        pltpu.make_async_copy(refs[i], refs[count + i], sems.at[i]) for i in range(count)
    ]
    for copy in copies:
        copy.start()
    for copy in copies:
        copy.wait()


_axis_order = ("dom", "rep")


def body(
    node_features, edge_features, node_cotangent, edge_cotangent,
    edge_in_weight, edge_in_bias, edge_out_weight, edge_out_bias,
    node_in_weight, node_in_bias, node_out_weight,
    edge_ends, live_elements, shared_nodes, shared_counts, multiplicity,
):
    n = lax.axis_size("dom")
    nodes, d = node_features.shape
    rows = edge_features.shape[0]
    edges = edge_ends.shape[1]
    s_count = shared_nodes.shape[2]
    hid = edge_in_weight.shape[1]
    edge_scale = 1.0 / math.sqrt(rows * n)
    node_scale = 1.0 / math.sqrt(nodes * n)
    slots = nodes // NPE
    quart = d // 4
    teams = n // 4
    vmem = pl.BlockSpec(memory_space=pltpu.VMEM)
    raw = pl.BlockSpec(memory_space=pl.ANY)
    hbm = pl.BlockSpec(memory_space=pltpu.HBM)
    shape = jax.ShapeDtypeStruct
    dma = pltpu.SemaphoreType.DMA
    vshape = pltpu.VMEM
    row = vshape((1, d), F32)
    args = (
        node_features, edge_features, node_cotangent, edge_cotangent,
        edge_in_weight, edge_in_bias.reshape(1, -1), edge_out_weight, edge_out_bias.reshape(1, -1),
        node_in_weight, node_in_bias.reshape(1, -1), node_out_weight,
        edge_ends, live_elements, shared_nodes[0], shared_counts,
        multiplicity.reshape(-1, LANES),
    )

    outs = pl.pallas_call(
        functools.partial(fused, n, n // 4, edge_scale, node_scale),
        out_shape=(
            vshape((nodes, d), BF16), vshape((rows, d), BF16),
            vshape((3 * d, hid), F32), row, vshape((hid, d), F32), row,
            vshape((2 * d, hid), F32), row, vshape((hid, d), F32), row,
        ),
        in_specs=[hbm] * 12 + [pl.BlockSpec(memory_space=pltpu.SMEM)] + [hbm] * 3,
        out_specs=(vmem,) * 10,
        scratch_shapes=[
            pltpu.VMEM((edges, LANES), F32), pltpu.VMEM((edges, LANES), F32),
            pltpu.VMEM((4 * s_count, LANES), F32), pltpu.VMEM((4, 8, s_count), F32),
            pltpu.VMEM((NPE, d), F32),
            pltpu.VMEM((edges, slots * d), BF16), pltpu.VMEM((edges, slots * d), BF16),
            pltpu.VMEM((edges, slots * hid), BF16), pltpu.VMEM((edges, slots * hid), F32),
            pltpu.VMEM((edges, slots * hid), F32), pltpu.VMEM((edges, slots * d), BF16),
            pltpu.VMEM((3 * slots * d, edges), BF16), pltpu.VMEM((edges, slots * hid), BF16),
            pltpu.VMEM((NPE, slots * hid), F32), pltpu.VMEM((2 * hid, nodes), BF16),
            pltpu.VMEM((2 * hid, 4 * s_count), BF16), pltpu.VMEM((hid, d), F32),
            pltpu.VMEM((nodes, d), BF16), pltpu.VMEM((NPE, slots * hid), F32),
            pltpu.VMEM((NPE, slots * hid), F32), pltpu.VMEM((nodes, d), F32),
            pltpu.VMEM((nodes, d), F32), pltpu.VMEM((nodes, d), F32),
        ]
        + [pltpu.VMEM((4, s_count, d), F32)] * 4
        + [pltpu.VMEM(arg.shape, arg.dtype) for i, arg in enumerate(args) if i != 12]
        + [dma((len(args) - 1,))]
        + [pltpu.VMEM((8, d), F32), pltpu.VMEM((n - 1, 8, d), F32)]
        + [dma((2,)), dma((2, 4)), dma, dma]
        + [
            pltpu.VMEM((7, 4, quart, d), F32), pltpu.VMEM((7, 3, quart, d), F32),
            pltpu.VMEM((7, quart, d), F32), pltpu.VMEM((7, teams - 1, quart, d), F32),
        ]
        + [dma, dma((7,)), dma, dma((7,)), dma, dma],
        compiler_params=pltpu.CompilerParams(
            collective_id=0, has_side_effects=True, vmem_limit_bytes=60 << 20
        ),
    )(*args)
    outs = pl.pallas_call(
        deliver,
        out_shape=tuple(shape(out.shape, out.dtype) for out in outs),
        in_specs=[vmem] * len(outs),
        out_specs=(raw,) * len(outs),
        scratch_shapes=[dma((len(outs),))],
        compiler_params=pltpu.CompilerParams(vmem_limit_bytes=8 << 20),
    )(*outs)
    flat = lambda v: v.reshape(-1)
    return (
        outs[0], outs[1], outs[2], flat(outs[3]), outs[4], flat(outs[5]),
        outs[6], flat(outs[7]), outs[8], flat(outs[9]),
    )


def solution(mesh):
    global _axis_order
    _axis_order = tuple(mesh.axis_names)
    both = P(("rep", "dom"))
    both2 = P(("rep", "dom"), None)
    in_specs = (
        (both2,) * 4 + (P(),) * 8 + (both, P(("rep", "dom"), None, None), both2, both)
    )
    out_specs = (both2, both2) + (P("rep", None), P("rep")) * 4
    return jax.shard_map(body, mesh=mesh, in_specs=in_specs, out_specs=out_specs, check_vma=False)
```

time: 45.3 us -> 40.2 us (0.89)
  Pallas kernels: 43.7 us -> 38.5 us
    pallas_call x1, Pallas kernels: 42.5 us -> 37.3 us  [body(): pl.pallas_call(functools.partial(fused, n, n // 4, edge_scale, node_scale...]
where the time goes in v2:
time: 40.2 us; the launch traced here: 39.9 us
  Pallas kernels  38.5 us (96%)
  between operations  1.46 us (4%)
    pallas_call x1, Pallas kernels, body(): pl.pallas_call(functools.partial(fused, n, n // 4, edge_scale, node_scale...  37.3 us
    pallas_call x1, Pallas kernels, body(): pl.pallas_call(deliver, out_shape=tuple((shape(out.shape, out.dtype) for...  1.18 us

profile of v2, /device:TPU:0, one launch (start us, length us, event | category | flops | bytes accessed | tf_op | source)
XLA Modules:
  0.0 39.9 jit_solution(1967118116100104695)
XLA Ops:
  1.3 37.3 %shard_map.231 = (bf16[1024,128]{1,0:T(8,128)(2,1)S(1)}, bf16[2688,128]{1,0:T(8,128)(2,1)S(1)}, f32[384,128]{1,0:T(8,128)S(1)}, f32[1,128]{1,0:T(1,128)S(1)}, f3...) custom-call(bf16[1024,128]{1,0:T(8,128)(2,1)} %nf_any.1, ...), custom_call_target="tpu_custom_call" | custom-call | tf_op jit(solution)/shard_map/pallas_call | solution.py:572
  38.6 1.2 %shard_map.232 = (bf16[1024,128]{1,0:T(8,128)(2,1)}, bf16[2688,128]{1,0:T(8,128)(2,1)}, f32[384,128]{1,0:T(8,128)}, f32[1,128]{1,0:T(1,128)}, f32[128,128]{1,0:T...) custom-call(bf16[1024,128]{1,0:T(8,128)(2,1)S(1)} %get-tuple-element, ...), custom_call_target="tpu_custom_call" | custom-call | tf_op jit(solution)/shard_map/pallas_call | solution.py:609

commit v3 on v2

--- a/solution.py
+++ b/solution.py
@@ -189,13 +189,15 @@
     w_in = jnp.concatenate([repeated(w, slots) for w in (ws, wt, we)], axis=0)
     bi_wide = twice(bi_ref[...])
 
-    for c in range(n_ch):
-        rows = slice(c * ch, (c + 1) * ch)
+    fwd = divisor_up_to(edges, 672)
+    n_fwd = edges // fwd
+    for c in range(n_fwd):
+        rows = slice(c * fwd, (c + 1) * fwd)
         target = mm(hits(col_t[rows, :], NPE), nf2).astype(BF16)
         source = mm(hits(col_s[rows, :], NPE), nf2).astype(BF16)
         src_s[rows, :] = source
         tgt_s[rows, :] = target
-        joined = jnp.concatenate([source, target, across(ef_ref, c * ch, ch, edges)], axis=1)
+        joined = jnp.concatenate([source, target, across(ef_ref, c * fwd, fwd, edges)], axis=1)
         hidden, slope = activation(mm2(joined, w_in) + bi_wide)
         hid_s[rows, :] = hidden.astype(BF16)
         slope_s[rows, :] = slope
@@ -462,6 +464,8 @@
     for at in (2, 1, 0):
         hold(6 - at, weigh(at))
         push(6 - at)
+    for p in range(0, 3):
+        cross(p)
     column = jnp.sum(eb_s[...].astype(F32), axis=0, keepdims=True)
     bias_row = column[:, :d]
     for e in range(1, slots):
@@ -496,16 +500,17 @@
             eg_ref[e * edges + c * ch : e * edges + (c + 1) * ch, :] = value[
                 :, e * d : (e + 1) * d
             ]
-    for p in range(0, 4):
-        cross(p)
+    cross(3)
     by_target = pair_of(by_row(mm2(row_hits(target_row, NPE, 1), eb2)))
     for p in range(4, 7):
         cross(p)
+    for p in range(0, 3):
+        share(p)
     by_source = pair_of(by_row(mm2(row_hits(source_row, NPE, 1), eb2)))
     w4 = jnp.concatenate([ws, ws, wt, wt], axis=1)
     spread = jnp.concatenate([by_source, by_target], axis=1)
     ng_ref[...] = (base_s[...] + mm_rt2(spread, w4)).astype(BF16)
-    for p in range(7):
+    for p in range(3, 7):
         share(p)
 
     whole(bias_l, bs_send, bs_recv).wait_recv()

time: 40.2 us -> 39.2 us (0.975)
  Pallas kernels: 38.5 us -> 37.4 us
    pallas_call x1, Pallas kernels: 37.3 us -> 36.3 us  [body(): pl.pallas_call(functools.partial(fused, n, n // 4, edge_scale, node_scale...]
where the time goes in v3:
time: 39.2 us; the launch traced here: 38.9 us
  Pallas kernels  37.4 us (95%)
  between operations  1.46 us (4%)
    pallas_call x1, Pallas kernels, body(): pl.pallas_call(functools.partial(fused, n, n // 4, edge_scale, node_scale...  36.3 us
    pallas_call x1, Pallas kernels, body(): pl.pallas_call(deliver, out_shape=tuple((shape(out.shape, out.dtype) for...  1.18 us

profile of v3, /device:TPU:0, one launch (start us, length us, event | category | flops | bytes accessed | tf_op | source)
XLA Modules:
  0.0 38.9 jit_solution(3134469791618001606)
XLA Ops:
  1.3 36.3 %shard_map.231 = (bf16[1024,128]{1,0:T(8,128)(2,1)S(1)}, bf16[2688,128]{1,0:T(8,128)(2,1)S(1)}, f32[384,128]{1,0:T(8,128)S(1)}, f32[1,128]{1,0:T(1,128)S(1)}, f3...) custom-call(bf16[1024,128]{1,0:T(8,128)(2,1)} %nf_any.1, ...), custom_call_target="tpu_custom_call" | custom-call | tf_op jit(solution)/shard_map/pallas_call | solution.py:577
  37.6 1.2 %shard_map.232 = (bf16[1024,128]{1,0:T(8,128)(2,1)}, bf16[2688,128]{1,0:T(8,128)(2,1)}, f32[384,128]{1,0:T(8,128)}, f32[1,128]{1,0:T(1,128)}, f32[128,128]{1,0:T...) custom-call(bf16[1024,128]{1,0:T(8,128)(2,1)S(1)} %get-tuple-element, ...), custom_call_target="tpu_custom_call" | custom-call | tf_op jit(solution)/shard_map/pallas_call | solution.py:614

commit v4 on v3

--- a/solution.py
+++ b/solution.py
@@ -265,7 +265,7 @@
             out[k] = fold(
                 mm(hits(lcol[k * s_count : (k + 1) * s_count, :], nodes, which), pair)
             )
-        for j in range(4):
+        for j in (0, 1, 3, 2):
             partner_copy(out, incoming, which, j).start()
 
     def landed(out, incoming, which, js):
@@ -335,7 +335,9 @@
     )
 
     def seat_of(i):
-        return lax.rem(seat + i, 4)
+        if i == 1:
+            return seat + 1 - 2 * lax.rem(seat, 2)
+        return lax.rem(seat + 2, 4) if i == 2 else 3 - seat
 
     def split_copy(p, i):
         return pltpu.make_async_remote_copy(
@@ -384,7 +386,7 @@
             qparts[p, j] = value[j * quart : (j + 1) * quart, :]
 
     def push(p):
-        for i in (2, 1, 3):
+        for i in (3, 2, 1):
             split_copy(p, i).start()
 
     def cross(p):
@@ -403,13 +405,15 @@
             total = total + clands[p, i]
         ref, first, scale = results[p]
         ref[pl.ds(pl.multiple_of(first + seat * quart, 8), quart), :] = total * scale
-        for i in (2, 1, 3):
+        for i in (3, 2, 1):
             share_copy(p, i).start()
 
     node_back = by_row(node_back2)
     hold(0, mm_lt2(nf_ref[...], node_back))
     hold(1, mm_lt2(consistent, node_back))
     hold(2, mm_lt2(by_row(node_hidden.astype(BF16)), cot_s[...]))
+    for p in range(3):
+        push(p)
     bias_s[2:3, :] = jnp.sum(node_back.astype(F32), axis=0, keepdims=True)
     base_s[...] = cot_s[...].astype(F32) + mm_rt2(node_back, wn[:d, :])
     wo_rows = jnp.concatenate([wo, wo], axis=1)
@@ -422,9 +426,6 @@
         got = mm(hits(col_t[rows, :], NPE, 1), pair_of(spread_back))
         lin_s[rows, :] = lin_s[rows, :] + got[:, :wide] + got[:, wide:]
 
-    for p in range(3):
-        push(p)
-
     def toward(moved, entries, e):
         wanted = entries - float(NPE * e)
         marks = jnp.concatenate(
@@ -434,7 +435,7 @@
             ],
             axis=1,
         )
-        return fold(mm(marks, moved))
+        return fold(mm2(marks, moved))
 
     moved, entries = landed(out2, in2, 1, near)
     moved = pair_of(mm_rt2(moved, wo_rows))
@@ -486,8 +487,6 @@
             device_id_type=MESH,
         )
 
-    lax.fori_loop(1, n, lambda i, x: (bias_copy(i).start(), x)[1], 0)
-
     eb2 = eb_s[...]
     we_wide = repeated(we, slots)
     quad = pair_of(by_slot(agg_back))
@@ -501,6 +500,8 @@
                 :, e * d : (e + 1) * d
             ]
     cross(3)
+    lax.fori_loop(1, n, lambda i, x: (bias_copy(i).start(), x)[1], 0)
+
     by_target = pair_of(by_row(mm2(row_hits(target_row, NPE, 1), eb2)))
     for p in range(4, 7):
         cross(p)
@@ -600,7 +601,7 @@
         + [pltpu.VMEM((4, s_count, d), F32)] * 4
         + [pltpu.VMEM(arg.shape, arg.dtype) for i, arg in enumerate(args) if i != 12]
         + [dma((len(args) - 1,))]
-        + [pltpu.VMEM((8, d), F32), pltpu.VMEM((n - 1, 8, d), F32)]
+        + [pltpu.VMEM((4, d), F32), pltpu.VMEM((n - 1, 4, d), F32)]
         + [dma((2,)), dma((2, 4)), dma, dma]
         + [
             pltpu.VMEM((7, 4, quart, d), F32), pltpu.VMEM((7, 3, quart, d), F32),

time: 39.2 us -> 38.4 us (0.980)
  Pallas kernels: 37.4 us -> 36.8 us
    pallas_call x1, Pallas kernels: 36.3 us -> 35.7 us  [body(): pl.pallas_call(functools.partial(fused, n, n // 4, edge_scale, node_scale...]
where the time goes in v4:
time: 38.4 us; the launch traced here: 38.1 us
  Pallas kernels  36.8 us (96%)
  between operations  1.3 us (3%)
    pallas_call x1, Pallas kernels, body(): pl.pallas_call(functools.partial(fused, n, n // 4, edge_scale, node_scale...  35.7 us
    pallas_call x1, Pallas kernels, body(): pl.pallas_call(deliver, out_shape=tuple((shape(out.shape, out.dtype) for...  1.18 us

profile of v4, /device:TPU:0, one launch (start us, length us, event | category | flops | bytes accessed | tf_op | source)
XLA Modules:
  0.0 38.1 jit_solution(5921690920522171989)
XLA Ops:
  1.3 35.7 %shard_map.231 = (bf16[1024,128]{1,0:T(8,128)(2,1)S(1)}, bf16[2688,128]{1,0:T(8,128)(2,1)S(1)}, f32[384,128]{1,0:T(8,128)S(1)}, f32[1,128]{1,0:T(1,128)S(1)}, f3...) custom-call(bf16[1024,128]{1,0:T(8,128)(2,1)} %nf_any.1, ...), custom_call_target="tpu_custom_call" | custom-call | tf_op jit(solution)/shard_map/pallas_call | solution.py:578
  37.0 1.2 %shard_map.232 = (bf16[1024,128]{1,0:T(8,128)(2,1)}, bf16[2688,128]{1,0:T(8,128)(2,1)}, f32[384,128]{1,0:T(8,128)}, f32[1,128]{1,0:T(1,128)}, f32[128,128]{1,0:T...) custom-call(bf16[1024,128]{1,0:T(8,128)(2,1)S(1)} %get-tuple-element, ...), custom_call_target="tpu_custom_call" | custom-call | tf_op jit(solution)/shard_map/pallas_call | solution.py:615

commit v5 on v4

--- a/solution.py
+++ b/solution.py
@@ -265,7 +265,7 @@
             out[k] = fold(
                 mm(hits(lcol[k * s_count : (k + 1) * s_count, :], nodes, which), pair)
             )
-        for j in (0, 1, 3, 2):
+        for j in ((1, 0, 3, 2), (0, 1, 3, 2))[which]:
             partner_copy(out, incoming, which, j).start()
 
     def landed(out, incoming, which, js):

time: 38.4 us -> 38.4 us (level)
  no operation moved by 1% of the time
where the time goes in v5:
time: 38.4 us; the launch traced here: 38.2 us
  Pallas kernels  36.8 us (96%)
  between operations  1.3 us (3%)
    pallas_call x1, Pallas kernels, body(): pl.pallas_call(functools.partial(fused, n, n // 4, edge_scale, node_scale...  35.7 us
    pallas_call x1, Pallas kernels, body(): pl.pallas_call(deliver, out_shape=tuple((shape(out.shape, out.dtype) for...  1.18 us

profile of v5, /device:TPU:0, one launch (start us, length us, event | category | flops | bytes accessed | tf_op | source)
XLA Modules:
  0.0 38.2 jit_solution(15377738164698449627)
XLA Ops:
  1.3 35.7 %shard_map.231 = (bf16[1024,128]{1,0:T(8,128)(2,1)S(1)}, bf16[2688,128]{1,0:T(8,128)(2,1)S(1)}, f32[384,128]{1,0:T(8,128)S(1)}, f32[1,128]{1,0:T(1,128)S(1)}, f3...) custom-call(bf16[1024,128]{1,0:T(8,128)(2,1)} %nf_any.1, ...), custom_call_target="tpu_custom_call" | custom-call | tf_op jit(solution)/shard_map/pallas_call | solution.py:578
  37.0 1.2 %shard_map.232 = (bf16[1024,128]{1,0:T(8,128)(2,1)}, bf16[2688,128]{1,0:T(8,128)(2,1)}, f32[384,128]{1,0:T(8,128)}, f32[1,128]{1,0:T(1,128)}, f32[128,128]{1,0:T...) custom-call(bf16[1024,128]{1,0:T(8,128)(2,1)S(1)} %get-tuple-element, ...), custom_call_target="tpu_custom_call" | custom-call | tf_op jit(solution)/shard_map/pallas_call | solution.py:615
